TPU v7x, 32 devices: a whole 2x2x4 slice. The times are simulated.
32 devices in a mesh: fsdp: 4 (over z), tensor: 2 (over core), pool: 4 (over y, x).
Axes of the slice: x: 2, y: 2, z: 4, core: 2. Of those that a mesh axis runs over, the one named last changes fastest.
Arguments:
- hidden: bfloat16 [8192, 5120], P(('fsdp', 'pool'), 'tensor'), may hold values from -6 to 6
- queries: bfloat16 [8192, 5120], P(('fsdp', 'pool'), 'tensor'), may hold values from -200 to 200
- cotangent: bfloat16 [8192, 5120], P(('fsdp', 'pool'), 'tensor'), may hold values from -6 to 6
- segment: int32 [16, 512], P(('fsdp', 'pool')), may hold values from 0 to 15, never falling along the last dimension, each value on 1 to 384 neighbouring positions
- clip_mask: int32 [8192], P(('fsdp', 'pool')), may hold values 0 or 1
- rewards: float32 [256], P(('fsdp', 'pool')), may hold values from 0 to 1
- seq_order: int32 [256], P(('fsdp', 'pool')), may hold values from 0 to 255, each once
- kv_weight: float32 [5120, 2, 1024], P('fsdp', None, 'tensor'), may hold values from -0.078125 to 0.078125
- moment_one: float32 [5120, 2, 1024], P('fsdp', None, 'tensor'), may hold values from -60 to 60
- moment_two: float32 [5120, 2, 1024], P('fsdp', None, 'tensor'), may hold values from 1 to 10000
- dec_hidden: bfloat16 [128, 4, 5120], P(('fsdp', 'pool')), may hold values from -6 to 6
- dec_queries: bfloat16 [128, 4, 5120], P(('fsdp', 'pool'), None, 'tensor'), may hold values from -200 to 200
- kv_cache: bfloat16 [128, 256, 2, 1024], P(('fsdp', 'pool'), None, None, 'tensor'), may hold values from -6 to 6
- cache_len: int32 [128], P(('fsdp', 'pool')), may hold values from 1 to 256
Outputs:
- new_weight: float32 [5120, 2, 1024], P('fsdp', None, 'tensor')
- new_moment_one: float32 [5120, 2, 1024], P('fsdp', None, 'tensor')
- new_moment_two: float32 [5120, 2, 1024], P('fsdp', None, 'tensor')
- dec_out: bfloat16 [128, 4, 5120], P(('fsdp', 'pool'), None, 'tensor')
Inputs may be any that keep to these rules, and one draw needn't show every extreme that they name: `segment`: each row never falls; every sequence number of a row has 1 to 384 tokens. `seq_order`: each place once.
All inputs are finite; a program needn't handle non-finite values. No bound on the sum of `clip_mask` on one device may be relied on, other than what follows from the above.
Results may differ from a plain program's by a relative error of at most 0.014.
The roundings to bfloat16 on the way count: a program that leaves them out, or rounds other values in their place, can miss the bound.
Values may be sent and summed in bfloat16 or wider, within the bound.
No kernel may reach another device: no remote copies, remote signals or barrier semaphores. Data moves between devices by JAX's collectives and lax.ppermute only.
A program may use at most 128 MiB of HBM per device.

v0:
```python
import math
import jax
import jax.numpy as jnp
from jax import lax
from jax.sharding import PartitionSpec as P

D = 5120
QH = 40
KVH = 8
HD = 128
GROUP = 16
beta_one = 0.9
beta_two = 0.999
learn_rate = 0.001
weight_decay = 0.1
adam_epsilon = 1e-08
adam_step = 10.0
variance_floor = 0.04
masked_score = -1e30


def learner_grads(keys_values, queries, cotangent, segment, coefficient):
    block_rows = queries.shape[0]
    head_size = queries.shape[3]
    score_scale = 1.0 / math.sqrt(head_size)
    key_rows = keys_values[:, 0]
    value_rows = keys_values[:, 1]
    scores = (
        jnp.einsum("thrd,uhd->hrtu", queries, key_rows, preferred_element_type=jnp.float32)
        * score_scale
    )
    places = jnp.arange(block_rows)
    allowed = (segment[:, None] == segment[None, :]) & (places[None, :] <= places[:, None])
    scores = jnp.where(allowed, scores, masked_score)
    row_max = jnp.max(scores, axis=-1, keepdims=True)
    weights = jnp.exp(scores - row_max)
    attention = weights / jnp.sum(weights, axis=-1, keepdims=True)
    attention_low = attention.astype(jnp.bfloat16)
    upstream = (coefficient[:, None, None, None] * cotangent.astype(jnp.float32)).astype(
        jnp.bfloat16
    )
    grad_prob = jnp.einsum(
        "thrd,uhd->hrtu", upstream, value_rows, preferred_element_type=jnp.float32
    )
    row_inner = jnp.sum(attention * grad_prob, axis=-1, keepdims=True)
    grad_score = (attention * (grad_prob - row_inner) * score_scale).astype(jnp.bfloat16)
    grad_values = jnp.einsum(
        "hrtu,thrd->uhd", attention_low, upstream, preferred_element_type=jnp.float32
    )
    grad_keys = jnp.einsum(
        "hrtu,thrd->uhd", grad_score, queries, preferred_element_type=jnp.float32
    )
    return jnp.stack([grad_keys, grad_values], axis=1).astype(jnp.bfloat16)


def decode_attend(queries, cache, fresh, lengths):
    head_size = queries.shape[4]
    steps_here = queries.shape[1]
    capacity = cache.shape[1]
    score_scale = 1.0 / math.sqrt(head_size)
    cached = (
        jnp.einsum("bshqd,blhd->bshql", queries, cache[:, :, 0], preferred_element_type=jnp.float32)
        * score_scale
    )
    recent = (
        jnp.einsum("bshqd,bjhd->bshqj", queries, fresh[:, :, 0], preferred_element_type=jnp.float32)
        * score_scale
    )
    live = jnp.arange(capacity)[None, :] < lengths[:, None]
    cached = jnp.where(live[:, None, None, None, :], cached, masked_score)
    before = jnp.arange(steps_here)[None, :] <= jnp.arange(steps_here)[:, None]
    recent = jnp.where(before[None, :, None, None, :], recent, masked_score)
    row_max = jnp.maximum(
        jnp.max(cached, axis=-1, keepdims=True), jnp.max(recent, axis=-1, keepdims=True)
    )
    cached_exp = jnp.exp(cached - row_max)
    recent_exp = jnp.exp(recent - row_max)
    total = jnp.sum(cached_exp, axis=-1, keepdims=True) + jnp.sum(
        recent_exp, axis=-1, keepdims=True
    )
    cached_low = (cached_exp / total).astype(jnp.bfloat16)
    recent_low = (recent_exp / total).astype(jnp.bfloat16)
    output = jnp.einsum(
        "bshql,blhd->bshqd", cached_low, cache[:, :, 1], preferred_element_type=jnp.float32
    )
    output = output + jnp.einsum(
        "bshqj,bjhd->bshqd", recent_low, fresh[:, :, 1], preferred_element_type=jnp.float32
    )
    return output.astype(jnp.bfloat16).reshape(queries.shape[0], steps_here, -1)


def body(
    hidden,
    queries,
    cotangent,
    segment,
    clip_mask,
    rewards,
    seq_order,
    kv_weight,
    moment_one,
    moment_two,
    dec_hidden,
    dec_queries,
    kv_cache,
    cache_len,
):
    block_rows = hidden.shape[0]
    kv_width = kv_weight.shape[2]
    heads_here = kv_width // HD
    head_ratio = QH // KVH
    weight_low = kv_weight.astype(jnp.bfloat16)
    weight_full = lax.all_gather(weight_low, "fsdp", axis=0, tiled=True)
    tokens_full = lax.all_gather(hidden, "tensor", axis=1, tiled=True)
    projected = jnp.dot(
        tokens_full, weight_full.reshape(D, 2 * kv_width), preferred_element_type=jnp.float32
    )
    keys_values = projected.astype(jnp.bfloat16).reshape(block_rows, 2, heads_here, HD)
    shards = lax.axis_size("fsdp") * lax.axis_size("pool")
    groups_total = rewards.shape[0] * shards // GROUP
    group_of = seq_order // GROUP
    onehot = (group_of[:, None] == jnp.arange(groups_total, dtype=jnp.int32)[None, :]).astype(
        jnp.float32
    )
    stats = jnp.stack([rewards, rewards * rewards], axis=1)
    partial_sums = jnp.sum(onehot[:, :, None] * stats[:, None, :], axis=0)
    sums = lax.psum(partial_sums, ("fsdp", "pool"))
    mean = sums[:, 0] / GROUP
    spread = sums[:, 1] / GROUP - mean * mean
    denom = jnp.sqrt(jnp.maximum(spread, variance_floor))
    advantage = (rewards - jnp.sum(onehot * mean[None, :], axis=1)) / jnp.sum(
        onehot * denom[None, :], axis=1
    )
    local_seg = segment[0]
    member = (local_seg[:, None] == jnp.arange(rewards.shape[0], dtype=jnp.int32)[None, :]).astype(
        jnp.float32
    )
    coefficient = jnp.sum(member * advantage[None, :], axis=1) * clip_mask.astype(jnp.float32)
    query_rows = queries.reshape(block_rows, heads_here, head_ratio, HD)
    cot_rows = cotangent.reshape(block_rows, heads_here, head_ratio, HD)
    grad_kv = learner_grads(keys_values, query_rows, cot_rows, local_seg, coefficient).reshape(
        block_rows, 2 * kv_width
    )
    partial_value = jnp.einsum(
        "tc,tk->ck", tokens_full, grad_kv, preferred_element_type=jnp.float32
    )
    shard_grad = lax.psum_scatter(
        partial_value.reshape(kv_weight.shape[0] * lax.axis_size("fsdp"), 2, kv_width).astype(
            jnp.bfloat16
        ),
        "fsdp",
        scatter_dimension=0,
        tiled=True,
    ).astype(jnp.float32)
    grad = lax.psum(shard_grad, "pool")
    new_moment_one = beta_one * moment_one + (1.0 - beta_one) * grad
    new_moment_two = beta_two * moment_two + (1.0 - beta_two) * grad * grad
    first_hat = new_moment_one / (1.0 - beta_one**adam_step)
    second_hat = new_moment_two / (1.0 - beta_two**adam_step)
    new_weight = kv_weight - learn_rate * (
        first_hat / (jnp.sqrt(second_hat) + adam_epsilon) + weight_decay * kv_weight
    )
    dec_rows = dec_hidden.shape[0]
    steps_here = dec_hidden.shape[1]
    capacity = kv_cache.shape[1]
    rollout_low = new_weight.astype(jnp.bfloat16)
    columns = lax.all_to_all(dec_hidden, "fsdp", split_axis=2, concat_axis=0, tiled=True)
    piece_width = columns.shape[2]
    rollout_flat = rollout_low.reshape(piece_width, 2 * kv_width)
    product = jnp.dot(
        columns.reshape(dec_rows * lax.axis_size("fsdp") * steps_here, piece_width),
        rollout_flat,
        preferred_element_type=jnp.float32,
    )
    fresh = lax.psum_scatter(
        product.reshape(dec_rows * lax.axis_size("fsdp"), steps_here, 2 * kv_width),
        "fsdp",
        scatter_dimension=0,
        tiled=True,
    )
    fresh_low = fresh.astype(jnp.bfloat16).reshape(dec_rows, steps_here, 2, heads_here, HD)
    cache = kv_cache.reshape(dec_rows, capacity, 2, heads_here, HD)
    query_dec = dec_queries.reshape(dec_rows, steps_here, heads_here, head_ratio, HD)
    dec_out = decode_attend(query_dec, cache, fresh_low, cache_len)
    return (new_weight, new_moment_one, new_moment_two, dec_out)


def solution(mesh):
    return jax.shard_map(
        body,
        mesh=mesh,
        in_specs=(
            P(("fsdp", "pool"), "tensor"),
            P(("fsdp", "pool"), "tensor"),
            P(("fsdp", "pool"), "tensor"),
            P(("fsdp", "pool"), None),
            P(("fsdp", "pool")),
            P(("fsdp", "pool")),
            P(("fsdp", "pool")),
            P("fsdp", None, "tensor"),
            P("fsdp", None, "tensor"),
            P("fsdp", None, "tensor"),
            P(("fsdp", "pool"), None, None),
            P(("fsdp", "pool"), None, "tensor"),
            P(("fsdp", "pool"), None, None, "tensor"),
            P(("fsdp", "pool")),
        ),
        out_specs=(
            P("fsdp", None, "tensor"),
            P("fsdp", None, "tensor"),
            P("fsdp", None, "tensor"),
            P(("fsdp", "pool"), None, "tensor"),
        ),
        check_vma=False,
    )
```

profile of v0, /device:TPU:0, one launch (start us, length us, event | category | flops | bytes accessed | tf_op | source)
XLA Modules:
  0.0 871.9 jit_solution(16252023753719787070)
XLA Ops:
  7.2 6.2 convert_element_type.64
  13.5 0.7 all-gather.3.cloned.1.call-update
  14.3 3.0 copy.102
  17.3 4.4 copy.99
  21.8 0.1 multiply_reduce_fusion
  21.9 45.7 %psum.14 = f32[16,2]{0,1:T(2,128)S(1)} all-reduce(f32[16,2]{0,1:T(2,128)S(1)} %multiply_reduce_fusion), channel_id=1, replica_groups=mesh['fsdp'=4,'tensor'=2,'pool'=4] {'fsdp','pool'}, use_global_device_ids=true, to_apply=%region_3.4 | all-reduce | flops 32 | bytes 256 | tf_op jit(solution)/shard_map/psum | solution.py:127
  67.6 0.2 select_reduce_fusion.2
  67.8 0.1 select_reduce_fusion
  67.9 0.2 fusion.56
  68.1 132.7 %all-gather.5.cloned.1.call-done = bf16[5120,2,512]{2,1,0:T(2,128)(2,1)} async-done(((bf16[1280,2,512]{2,1,0:T(2,128)(2,1)}), bf16[5120,2,512]{2,1,0:T(2,128)(2,1)}) %all-gather.5.cloned.1.call-update) | async-done | bytes 10485776 | tf_op jit(solution)/shard_map/all_gather | solution.py:113
  200.8 12.6 %copy.142 = bf16[640,8,2,512]{3,1,2,0:T(8,128)(2,1)} copy(bf16[640,8,2,512]{3,2,1,0:T(2,128)(2,1)} %bitcast.179) | data formatting | bytes 20971520
  213.4 2.4 all-gather.3.cloned.1.call-done
  215.8 10.6 %convolution_convert_fusion.1 = bf16[512,1024]{1,0:T(8,128)(2,1)} fusion(bf16[512,5120]{1,0:T(8,128)(2,1)} %all-gather.3.cloned.1.call-done, bf16[5120,1024]{1,0:T(8,128)(2,1)} %bitcast.180), kind=kOutput, calls=%fused_computation.33 | convolution fusion | flops 5369233408 | bytes 16777216 | tf_op jit(solution)/shard_map/dot_general | solution.py:115
  226.4 2.6 reshape.138
  229.0 1.6 fusion.75
  230.6 8.5 fusion.18
  239.0 13.0 %fusion.77 = (f32[4,5,512]{2,1,0:T(8,128)S(1)}, f32[4,5,512,512]{2,3,1,0:T(8,128)}) fusion(pred[512,512]{0,1:T(8,128)(4,1)S(1)} %fusion.56, bf16[512,4,5,128]{0,3,2,1:T(8,128)(2,1)} %bitcast.187, bf16[512,1,4,128]{3,2,1,0:T(4,128)(2,1)S(1)} %get-tuple-element.27), kind=kOutput, calls=%fused_computation.99 | convolution fusion | flops 1363149312 | bytes 24420352 | tf_op jit(solution)/shard_map/sub | solution.py:36
  252.1 8.9 %fusion.43 = bf16[512,1,4,128]{0,3,2,1:T(8,128)(2,1)S(1)} fusion(bf16[512,4,5,128]{0,3,2,1:T(8,128)(2,1)S(1)} %bitcast.184, f32[512]{0:T(512)S(1)} %convert_multiply_fusion.1, f32[4,5,512,512]{2,3,1,0:T(8,128)} %get-tuple-element.31, f32[4,5,512]{2,1,0:T(8,128)S(1)} %get-tuple-element.30), kind=kOutput, calls=%fused_computation.41 | convolution fusion | flops 1356857344 | bytes 24160256 | tf_op jit(solution)/shard_map/hrtu,thrd->uhd/dot_general | solution.py:47
  261.0 27.9 %fusion.48 = bf16[512,1,4,128]{0,3,2,1:T(8,128)(2,1)S(1)} fusion(bf16[512,4,5,128]{0,3,2,1:T(8,128)(2,1)} %bitcast.188, f32[4,512,512,5]{2,1,3,0:T(8,128)} %fusion.18, f32[4,5,512,512]{2,3,1,0:T(8,128)} %get-tuple-element.31, f32[4,5,512]{2,1,0:T(8,128)S(1)} %get-tuple-element.30), kind=kOutput, calls=%fused_computation.42 | convolution fusion | flops 1379150336 | bytes 45129728 | tf_op jit(solution)/shard_map/hrtu,thrd->uhd/dot_general | solution.py:50
  288.9 0.1 pad_maximum_fusion
  289.0 10.8 %convolution_convert_fusion = bf16[1024,5120]{1,0:T(8,128)(2,1)} fusion(bf16[512,1024]{0,1:T(8,128)(2,1)S(1)} %bitcast.190, bf16[512,5120]{1,0:T(8,128)(2,1)} %all-gather.3.cloned.1.call-done), kind=kOutput, calls=%fused_computation.18 | convolution fusion | flops 5373952000 | bytes 16777216 | tf_op jit(solution)/shard_map/tc,tk->ck/dot_general | solution.py:144
  299.8 26.0 %copy.106 = bf16[5120,2,512]{2,1,0:T(2,128)(2,1)} copy(bf16[5120,2,512]{0,2,1:T(8,128)(2,1)} %bitcast.181) | data formatting | bytes 20971520 | tf_op jit(solution)/shard_map/convert_element_type | solution.py:148
  325.9 0.6 copy-done.7
  326.5 0.6 dynamic-slice
  327.8 357.9 %all-reduce.6.cloned.1.call-done = bf16[5120,2,512]{2,1,0:T(2,128)(2,1)} async-done(((bf16[5120,2,512]{2,1,0:T(2,128)(2,1)}), bf16[5120,2,512]{2,1,0:T(2,128)(2,1)}) %all-reduce.6.cloned.1.call-update) | async-done | bytes 10485776
  685.7 6.0 dynamic-slice_convert_fusion
  691.8 5.0 copy.111
  696.7 6.9 reshape.159
  703.6 12.9 %all_to_all.15 = bf16[4,2,20480]{2,1,0:T(2,128)(2,1)S(1)} all-to-all(bf16[4,2,20480]{2,1,0:T(2,128)(2,1)S(1)} %reshape.159), channel_id=1, replica_groups=mesh['fsdp'=4,'tensor'=2,'pool'=4] {'fsdp'}, dimensions={0} | all-to-all | bytes 655360 | tf_op jit(solution)/shard_map/all_to_all | solution.py:167
  716.6 7.2 reshape.160
  723.8 6.7 copy.112
  730.6 81.1 %all-reduce.4.cloned.1.call-done = f32[1280,2,512]{2,1,0:T(2,128)} async-done(((f32[1280,2,512]{2,1,0:T(2,128)}), f32[1280,2,512]{2,1,0:T(2,128)}) %all-reduce.4.cloned.1.call-update) | async-done | bytes 5242896 | tf_op jit(solution)/shard_map/psum | solution.py:155
  811.7 22.5 %fusion.73 = (bf16[1280,2,512]{2,1,0:T(2,128)(2,1)S(1)}, f32[1280,2,512]{2,1,0:T(2,128)}, f32[1280,2,512]{2,1,0:T(2,128)}, f32[1280,2,512]{2,1,0:T(2,128)}) fusion(f32[1280,2,512]{2,1,0:T(2,128)} %param.21, f32[1280,2,512]{2,1,0:T(2,128)} %all-reduce.4.cloned.1.call-done, f32[1280,2,512]{2,1,0:T(2,128)} %param.22, f32[1280,2,512]{2,1,0:T(2,128)} %param.23), kind=kLoop, calls=%fused_computation.96 | loop fusion | flops 20971520 | bytes 39321600 | tf_op jit(solution)/shard_map/convert_element_type | solution.py:166
  834.2 0.7 copy.143
  834.9 0.5 convolution_bitcast_fusion.1
  835.4 0.1 reshape.144
  835.6 1.1 copy.113
  836.7 0.2 reshape.158
  836.9 11.1 %copy.107 = bf16[8,256,2,512]{1,3,2,0:T(8,128)(2,1)} copy(bf16[8,256,2,512]{3,2,1,0:T(2,128)(2,1)} %param.26) | data formatting | bytes 8388608 | tf_op args[12]
  848.1 2.1 fusion.78
  850.2 8.5 reduce-scatter.2.cloned.1.call-done
  858.7 0.9 convert_element_type.79
  859.7 1.3 fusion.79
  861.0 0.2 fusion.63
  861.3 0.5 fusion.57
  861.8 2.3 fusion.51
  864.1 0.4 fusion.53
  864.6 0.8 reshape.156
  (40 shorter events, 0.7 us)
Async XLA Ops:
  7.2 193.7 %all-gather.5.cloned.1.call-start = ((), (), s32[]{:S(2)}) async-start(), calls=%async_computation.3 | async-start | bytes 13107200 | tf_op jit(solution)/shard_map/all_gather | solution.py:113
  13.4 202.4 %all-gather.3.cloned.1.call-start = ((), (), s32[]{:S(2)}) async-start(), calls=%async_computation.2 | async-start | bytes 7864320 | tf_op jit(solution)/shard_map/all_gather | solution.py:114
  14.2 7.5 copy-start.4
  14.2 7.5 copy-start.6
  14.2 53.6 %copy-start.2 = (s32[1,512]{1,0:T(1,128)S(1)}, s32[1,512]{1,0:T(1,128)}, u32[]{:S(2)}) copy-start(s32[1,512]{1,0:T(1,128)} %param.17) | copy-start | bytes 6148
  14.2 53.7 %copy-start.3 = (s32[512]{0:T(512)S(1)}, s32[512]{0:T(512)}, u32[]{:S(2)}) copy-start(s32[512]{0:T(512)} %param.18) | copy-start | bytes 6148
  14.2 671.5 %all-reduce.6.cloned.1.call-start = ((), (), s32[]{:S(2)}) async-start(), calls=%async_computation.6 | async-start | bytes 20971520
  325.9 0.7 copy-start.7
  325.9 485.8 %all-reduce.4.cloned.1.call-start = ((), (), s32[]{:S(2)}) async-start(), calls=%async_computation.4 | async-start | bytes 10485760 | tf_op jit(solution)/shard_map/psum | solution.py:155
  327.8 364.0 %copy-start = (bf16[8,4,5120]{2,1,0:T(4,128)(2,1)S(1)}, bf16[8,4,5120]{2,1,0:T(4,128)(2,1)}, u32[]{:S(2)}) copy-start(bf16[8,4,5120]{2,1,0:T(4,128)(2,1)} %param.24) | copy-start | bytes 983044
  691.7 167.0 %reduce-scatter.2.cloned.1.call-start = ((), (), s32[]{:S(2)}) async-start(), calls=%async_computation.5 | async-start | bytes 655360 | tf_op jit(solution)/shard_map/reduce_scatter | solution.py:175
  834.2 2.5 copy-start.1
  835.6 12.4 %copy-start.5 = (s32[8]{0:T(128)S(1)}, s32[8]{0:T(128)}, u32[]{:S(2)}) copy-start(s32[8]{0:T(128)} %param.27) | copy-start | bytes 100
Sparse Core Ops, SparseCore 0:
  13.5 187.2 all-gather.4
  202.4 13.4 all-gather.2
  326.0 359.6 all-reduce.5
  691.8 119.8 all-reduce.3
  836.9 21.8 reduce-scatter.1
where the time goes:
time: 874 us; the launch traced here: 872 us
  waiting for transfers between devices  583 us (67%)
  local copies, waits for them, and re-layouts  91.3 us (10%)
  matrix products  86.4 us (10%)
  blocking collectives  58.7 us (7%)
  other arithmetic  37.2 us (4%)
  between operations  14.7 us (2%)
    unnamed x6, waiting for transfers between devices  359 us
    all_gather x1, waiting for transfers between devices, body(): weight_full = lax.all_gather(weight_low, 'fsdp', axis=0, tiled=True)  133 us
    psum x1, waiting for transfers between devices, body(): grad = lax.psum(shard_grad, 'pool')  81.1 us
    unnamed x27, local copies, waits for them, and re-layouts  52.8 us
    psum x1, blocking collectives, body(): sums = lax.psum(partial_sums, ('fsdp', 'pool'))  45.7 us
    dot_general x1, matrix products, learner_grads(): jnp.einsum('hrtu,thrd->uhd', grad_score, queries, preferred_element_type=...  27.9 us
    convert_element_type x1, local copies, waits for them, and re-layouts, body(): partial_value.reshape(kv_weight.shape[0] * lax.axis_size('fsdp'), 2, kv_w...  26 us
    convert_element_type x1, other arithmetic, body(): rollout_low = new_weight.astype(jnp.bfloat16)  22.5 us
  transfers between devices with their start and end apart: 5, of which 5 were waited for; matrix products, arithmetic and copies ran while one was open for 7% of the time, Pallas kernels for 0%

commit v1 on v0

--- a/solution.py
+++ b/solution.py
@@ -152,7 +152,7 @@
         scatter_dimension=0,
         tiled=True,
     ).astype(jnp.float32)
-    grad = lax.psum(shard_grad, "pool")
+    grad = jnp.sum(lax.all_gather(shard_grad, "pool"), axis=0)
     new_moment_one = beta_one * moment_one + (1.0 - beta_one) * grad
     new_moment_two = beta_two * moment_two + (1.0 - beta_two) * grad * grad
     first_hat = new_moment_one / (1.0 - beta_one**adam_step)

time: 874 us -> 794 us (0.908)
  waiting for transfers between devices: 583 us -> 451 us
  local copies, waits for them, and re-layouts: 91.3 us -> 142 us
  blocking collectives: 58.7 us -> 45.7 us
  other arithmetic: 37.2 us -> 46.1 us
    unnamed x6 -> x5, waiting for transfers between devices: 359 us -> 0.76 us
    reduce_scatter x0 -> x1, waiting for transfers between devices: none -> 179 us  [body(): lax.psum_scatter(partial_value.reshape(kv_weight.shape[0] * lax.axis_size...]
    all_gather x0 -> x1, waiting for transfers between devices: none -> 136 us  [body(): grad = jnp.sum(lax.all_gather(shard_grad, 'pool'), axis=0)]
    psum x1 -> x0, waiting for transfers between devices: 81.1 us -> none  [body(): grad = lax.psum(shard_grad, 'pool')]
    unnamed x27 -> x29, local copies, waits for them, and re-layouts: 52.8 us -> 104 us
    convert_element_type x1 -> x0, local copies, waits for them, and re-layouts: 26 us -> none  [body(): partial_value.reshape(kv_weight.shape[0] * lax.axis_size('fsdp'), 2, kv_w...]
    all_gather x0 -> x1, local copies, waits for them, and re-layouts: none -> 25.3 us  [body(): grad = jnp.sum(lax.all_gather(shard_grad, 'pool'), axis=0)]
    reduce_sum x0 -> x1, other arithmetic: none -> 18.5 us  [body(): grad = jnp.sum(lax.all_gather(shard_grad, 'pool'), axis=0)]
  transfers between devices with their start and end apart: 5 -> 6, of which waited for: 5 -> 4; matrix products, arithmetic and copies ran while one was open for 7% -> 14% of each run, Pallas kernels for 0% -> 0%
where the time goes in v1:
time: 794 us; the launch traced here: 791 us
  waiting for transfers between devices  451 us (57%)
  local copies, waits for them, and re-layouts  142 us (18%)
  matrix products  86.9 us (11%)
  other arithmetic  46.1 us (6%)
  blocking collectives  45.7 us (6%)
  between operations  14 us (2%)
    reduce_scatter x1, waiting for transfers between devices, body(): lax.psum_scatter(partial_value.reshape(kv_weight.shape[0] * lax.axis_size...  179 us
    all_gather x1, waiting for transfers between devices, body(): grad = jnp.sum(lax.all_gather(shard_grad, 'pool'), axis=0)  136 us
    all_gather x1, waiting for transfers between devices, body(): weight_full = lax.all_gather(weight_low, 'fsdp', axis=0, tiled=True)  133 us
    unnamed x29, local copies, waits for them, and re-layouts  104 us
    psum x1, blocking collectives, body(): sums = lax.psum(partial_sums, ('fsdp', 'pool'))  45.7 us
    dot_general x1, matrix products, learner_grads(): jnp.einsum('hrtu,thrd->uhd', grad_score, queries, preferred_element_type=...  27.9 us
    all_gather x1, local copies, waits for them, and re-layouts, body(): grad = jnp.sum(lax.all_gather(shard_grad, 'pool'), axis=0)  25.3 us
    reduce_sum x1, other arithmetic, body(): grad = jnp.sum(lax.all_gather(shard_grad, 'pool'), axis=0)  18.5 us
  transfers between devices with their start and end apart: 6, of which 4 were waited for; matrix products, arithmetic and copies ran while one was open for 14% of the time, Pallas kernels for 0%

profile of v1, /device:TPU:0, one launch (start us, length us, event | category | flops | bytes accessed | tf_op | source)
XLA Modules:
  0.0 791.1 jit_solution(3759210770665864972)
XLA Ops:
  7.2 6.2 convert_element_type.62
  13.5 0.7 all-gather.5.cloned.1.call-update
  14.3 3.0 copy.113
  17.3 4.4 copy.110
  21.9 45.7 %psum.7 = f32[16,2]{0,1:T(2,128)S(1)} all-reduce(f32[16,2]{0,1:T(2,128)S(1)} %multiply_reduce_fusion), channel_id=1, replica_groups=mesh['fsdp'=4,'tensor'=2,'pool'=4] {'fsdp','pool'}, use_global_device_ids=true, to_apply=%region_3.4 | all-reduce | flops 32 | bytes 256 | tf_op jit(solution)/shard_map/psum | solution.py:127
  67.6 0.2 select_reduce_fusion.2
  67.9 0.2 fusion.56
  68.1 132.7 %all-gather.7.cloned.1.call-done = bf16[5120,2,512]{2,1,0:T(2,128)(2,1)} async-done(((bf16[1280,2,512]{2,1,0:T(2,128)(2,1)}), bf16[5120,2,512]{2,1,0:T(2,128)(2,1)}) %all-gather.7.cloned.1.call-update) | async-done | bytes 10485776 | tf_op jit(solution)/shard_map/all_gather | solution.py:113
  200.8 12.6 %copy.158 = bf16[640,8,2,512]{3,1,2,0:T(8,128)(2,1)} copy(bf16[640,8,2,512]{3,2,1,0:T(2,128)(2,1)} %bitcast.179) | data formatting | bytes 20971520
  213.4 2.4 all-gather.5.cloned.1.call-done
  215.8 10.6 %convolution_convert_fusion.1 = bf16[512,1024]{1,0:T(8,128)(2,1)} fusion(bf16[512,5120]{1,0:T(8,128)(2,1)} %all-gather.5.cloned.1.call-done, bf16[5120,1024]{1,0:T(8,128)(2,1)} %bitcast.181), kind=kOutput, calls=%fused_computation.32 | convolution fusion | flops 5369233408 | bytes 16777216 | tf_op jit(solution)/shard_map/dot_general | solution.py:115
  226.4 2.6 reshape.138
  229.0 1.6 fusion.75
  230.6 8.5 %fusion.18 = f32[4,512,512,5]{2,1,3,0:T(8,128)} fusion(bf16[512,4,5,128]{0,3,2,1:T(8,128)(2,1)S(1)} %bitcast.182, f32[512]{0:T(512)S(1)} %convert_multiply_fusion.1, bf16[512,1,4,128]{3,2,1,0:T(4,128)(2,1)S(1)} %get-tuple-element.26), kind=kOutput, calls=%fused_computation.26 | convolution fusion | flops 1346109440 | bytes 24119296 | tf_op jit(solution)/shard_map/thrd,uhd->hrtu/dot_general | solution.py:42
  239.0 13.0 %fusion.77 = (f32[4,5,512]{2,1,0:T(8,128)S(1)}, f32[4,5,512,512]{2,3,1,0:T(8,128)}) fusion(pred[512,512]{0,1:T(8,128)(4,1)S(1)} %fusion.56, bf16[512,4,5,128]{0,3,2,1:T(8,128)(2,1)} %bitcast.186, bf16[512,1,4,128]{3,2,1,0:T(4,128)(2,1)S(1)} %get-tuple-element.27), kind=kOutput, calls=%fused_computation.98 | convolution fusion | flops 1363149312 | bytes 24420352 | tf_op jit(solution)/shard_map/sub | solution.py:36
  252.1 8.9 %fusion.43 = bf16[512,1,4,128]{0,3,2,1:T(8,128)(2,1)S(1)} fusion(bf16[512,4,5,128]{0,3,2,1:T(8,128)(2,1)S(1)} %bitcast.183, f32[512]{0:T(512)S(1)} %convert_multiply_fusion.1, f32[4,5,512,512]{2,3,1,0:T(8,128)} %get-tuple-element.31, f32[4,5,512]{2,1,0:T(8,128)S(1)} %get-tuple-element.30), kind=kOutput, calls=%fused_computation.40 | convolution fusion | flops 1356857344 | bytes 24160256 | tf_op jit(solution)/shard_map/hrtu,thrd->uhd/dot_general | solution.py:47
  261.0 27.9 %fusion.48 = bf16[512,1,4,128]{0,3,2,1:T(8,128)(2,1)S(1)} fusion(bf16[512,4,5,128]{0,3,2,1:T(8,128)(2,1)} %bitcast.187, f32[4,512,512,5]{2,1,3,0:T(8,128)} %fusion.18, f32[4,5,512,512]{2,3,1,0:T(8,128)} %get-tuple-element.31, f32[4,5,512]{2,1,0:T(8,128)S(1)} %get-tuple-element.30), kind=kOutput, calls=%fused_computation.41 | convolution fusion | flops 1379150336 | bytes 45129728 | tf_op jit(solution)/shard_map/hrtu,thrd->uhd/dot_general | solution.py:50
  289.0 10.8 %convolution_convert_fusion = bf16[1024,5120]{1,0:T(8,128)(2,1)} fusion(bf16[512,1024]{0,1:T(8,128)(2,1)S(1)} %bitcast.189, bf16[512,5120]{1,0:T(8,128)(2,1)} %all-gather.5.cloned.1.call-done), kind=kOutput, calls=%fused_computation.18 | convolution fusion | flops 5373952000 | bytes 16777216 | tf_op jit(solution)/shard_map/tc,tk->ck/dot_general | solution.py:144
  299.9 179.3 %reduce-scatter.3.cloned.1.call-done = bf16[1280,2,512]{0,2,1:T(8,128)(2,1)} async-done(((bf16[5120,2,512]{0,2,1:T(8,128)(2,1)}), bf16[1280,2,512]{0,2,1:T(8,128)(2,1)}) %reduce-scatter.3.cloned.1.call-update) | async-done | bytes 2621456 | tf_op jit(solution)/shard_map/reduce_scatter | solution.py:147
  479.2 4.5 all_gather.20
  483.8 5.0 copy.124
  488.7 7.9 %reshape.160 = bf16[4,2,20480]{2,1,0:T(2,128)(2,1)} reshape(bf16[5120,4,8]{2,1,0:T(4,128)(2,1)} %bitcast.177) | data formatting | bytes 655360
  496.7 4.7 all-to-all-start
  501.4 8.8 %copy.119 = f32[1280,2,512]{0,2,1:T(8,128)} copy(f32[1280,2,512]{2,1,0:T(2,128)} %param.21) | data formatting | bytes 10485760 | tf_op args[7]
  510.2 8.7 %copy.108 = f32[1280,2,512]{0,2,1:T(8,128)} copy(f32[1280,2,512]{2,1,0:T(2,128)} %param.22) | data formatting | bytes 10485760 | tf_op args[8]
  518.8 8.9 %copy.117 = f32[1280,2,512]{0,2,1:T(8,128)} copy(f32[1280,2,512]{2,1,0:T(2,128)} %param.23) | data formatting | bytes 10485760 | tf_op args[9]
  527.7 7.3 reshape.161
  535.0 6.7 copy.125
  541.7 136.3 %all-gather.9.cloned.1.call-done = f32[5120,2,512]{0,2,1:T(8,128)} async-done(((f32[1280,2,512]{0,2,1:T(8,128)}), f32[5120,2,512]{0,2,1:T(8,128)}) %all-gather.9.cloned.1.call-update) | async-done | bytes 20971536 | tf_op jit(solution)/shard_map/all_gather | solution.py:155
  678.0 25.3 %reshape.149 = f32[4,1280,2,512]{1,0,3,2:T(4,128)} reshape(f32[5120,2,512]{0,2,1:T(8,128)} %all-gather.9.cloned.1.call-done) | data formatting | bytes 41943040 | tf_op jit(solution)/shard_map/all_gather | solution.py:155
  703.3 18.5 %reduce_sum.87 = f32[1280,2,512]{0,2,1:T(8,128)} reduce(f32[4,1280,2,512]{1,0,3,2:T(4,128)} %reshape.149, f32[]{:T(128)} %constant.37.clone.1), dimensions={0}, to_apply=%region_9.10 | reduce | flops 3932160 | bytes 26214404 | tf_op jit(solution)/shard_map/reduce_sum | solution.py:155
  721.8 14.3 %fusion.73 = (bf16[1280,2,512]{0,2,1:T(8,128)(2,1)S(1)}, f32[1280,2,512]{0,2,1:T(8,128)}, f32[1280,2,512]{0,2,1:T(8,128)}, f32[1280,2,512]{0,2,1:T(8,128)}) fusion(f32[1280,2,512]{0,2,1:T(8,128)} %copy.119, f32[1280,2,512]{0,2,1:T(8,128)} %reduce_sum.87, f32[1280,2,512]{0,2,1:T(8,128)} %copy.108, f32[1280,2,512]{0,2,1:T(8,128)} %copy.117), kind=kLoop, calls=%fused_computation.95 | loop fusion | flops 20971520 | bytes 39321600 | tf_op jit(solution)/shard_map/convert_element_type | solution.py:166
  736.1 1.0 convolution_bitcast_fusion.1
  737.1 0.1 reshape.144
  737.3 1.1 copy.126
  738.4 0.2 reshape.159
  738.6 11.1 %copy.120 = bf16[8,256,2,512]{1,3,2,0:T(8,128)(2,1)} copy(bf16[8,256,2,512]{3,2,1,0:T(2,128)(2,1)} %param.26) | data formatting | bytes 8388608 | tf_op args[12]
  749.8 2.1 fusion.78
  751.9 8.7 %copy.132 = f32[1280,2,512]{2,1,0:T(2,128)} copy(f32[1280,2,512]{0,2,1:T(8,128)} %get-tuple-element.23) | data formatting | bytes 10485760
  760.6 8.7 %copy.133 = f32[1280,2,512]{2,1,0:T(2,128)} copy(f32[1280,2,512]{0,2,1:T(8,128)} %get-tuple-element.24) | data formatting | bytes 10485760
  769.3 8.7 %copy.134 = f32[1280,2,512]{2,1,0:T(2,128)} copy(f32[1280,2,512]{0,2,1:T(8,128)} %get-tuple-element.25) | data formatting | bytes 10485760
  778.0 0.9 convert_element_type.76
  779.0 1.3 fusion.79
  780.3 0.2 fusion.63
  780.6 0.5 fusion.57
  781.1 2.3 fusion.51
  783.4 0.4 fusion.53
  783.8 0.8 reshape.158
  (44 shorter events, 1.0 us)
Async XLA Ops:
  7.2 193.7 %all-gather.7.cloned.1.call-start = ((), (), s32[]{:S(2)}) async-start(), calls=%async_computation.4 | async-start | bytes 13107200 | tf_op jit(solution)/shard_map/all_gather | solution.py:113
  13.4 202.4 %all-gather.5.cloned.1.call-start = ((), (), s32[]{:S(2)}) async-start(), calls=%async_computation.3 | async-start | bytes 7864320 | tf_op jit(solution)/shard_map/all_gather | solution.py:114
  14.2 7.5 copy-start.4
  14.2 7.5 copy-start.6
  14.2 53.6 %copy-start.2 = (s32[1,512]{1,0:T(1,128)S(1)}, s32[1,512]{1,0:T(1,128)}, u32[]{:S(2)}) copy-start(s32[1,512]{1,0:T(1,128)} %param.17) | copy-start | bytes 6148
  14.2 53.7 %copy-start.3 = (s32[512]{0:T(512)S(1)}, s32[512]{0:T(512)}, u32[]{:S(2)}) copy-start(s32[512]{0:T(512)} %param.18) | copy-start | bytes 6148
  14.2 465.0 %reduce-scatter.3.cloned.1.call-start = ((), (), s32[]{:S(2)}) async-start(), calls=%async_computation.5 | async-start | bytes 13107200 | tf_op jit(solution)/shard_map/reduce_scatter | solution.py:147
  299.9 183.9 %copy-start = (bf16[8,4,5120]{2,1,0:T(4,128)(2,1)S(1)}, bf16[8,4,5120]{2,1,0:T(4,128)(2,1)}, u32[]{:S(2)}) copy-start(bf16[8,4,5120]{2,1,0:T(4,128)(2,1)} %param.24) | copy-start | bytes 983044
  299.9 378.1 %all-gather.9.cloned.1.call-start = ((), (), s32[]{:S(2)}) async-start(), calls=%async_computation.7 | async-start | bytes 26214400 | tf_op jit(solution)/shard_map/all_gather | solution.py:155
  496.7 31.1 %all-to-all-start = ((bf16[4,2,20480]{2,1,0:T(2,128)(2,1)}), bf16[4,2,20480]{2,1,0:T(2,128)(2,1)S(1)}, u32[]{:S(2)}, u32[]{:S(2)}) async-start(bf16[4,2,20480]{2,1,0:T(2,128)(2,1)} %reshape.160), calls=%async_computation.1 | async-start | bytes 655360 | tf_op jit(solution)/shard_map/all_to_all | solution.py:167
  501.4 276.6 %reduce-scatter.5.cloned.1.call-start = ((), (), s32[]{:S(2)}) async-start(), calls=%async_computation.6 | async-start | bytes 655360 | tf_op jit(solution)/shard_map/reduce_scatter | solution.py:175
  736.1 2.3 copy-start.1
  737.3 12.4 %copy-start.5 = (s32[8]{0:T(128)S(1)}, s32[8]{0:T(128)}, u32[]{:S(2)}) copy-start(s32[8]{0:T(128)} %param.27) | copy-start | bytes 100
Sparse Core Ops, SparseCore 0:
  13.5 187.2 all-gather.6
  202.4 13.4 all-gather.4
  300.0 179.2 reduce-scatter.2
  483.9 194.0 all-gather.8
  738.5 21.8 reduce-scatter.4
